TPU v7x, 512 devices: a whole 4x4x16 slice. The times are simulated.
512 devices in a mesh: strata: 32 (over z, x_lo), shard: 16 (over y, x_hi, core).
Axes of the slice: x: 4 (x_hi: 2, x_lo: 2; x = x_hi * 2 + x_lo), y: 4, z: 16, core: 2. Of those that a mesh axis runs over, the one named last changes fastest.
Arguments:
- user_factors: bfloat16 [524288, 512], P(('strata', 'shard')), may hold values from -1.1953125 to 1.1953125
- item_factors: float32 [16384, 512], P(('strata', 'shard')), may hold values from -1.2 to 1.2
- tile_blocks: int32 [32, 16, 3, 8, 2], P('strata', 'shard'), may hold values from 0 to 7, as said below
- tile_counts: int32 [32, 16, 3], P('strata', 'shard'), may hold values from 1 to 8, as said below
- ratings: bfloat16 [32, 16, 3, 8, 128, 128], P('strata', 'shard'), may hold values from -5 to 5
- mask_words: int32 [32, 16, 3, 8, 16, 128], P('strata', 'shard'), may hold values from 0 to 255
Outputs:
- users_out: bfloat16 [524288, 512], P(('strata', 'shard'))
- items_out: float32 [16384, 512], P(('strata', 'shard'))
Inputs may be any that keep to these rules, and one draw needn't show every extreme that they name: `tile_blocks`: entry 0 is a user block below 8, entry 1 an item block below 4; the 8 pairs of one stratum, shard and visit are distinct. `tile_counts`: some stratum, shard and visit has exactly 8 live slots in every draw.
All inputs are finite; a program needn't handle non-finite values.
Results may differ from a plain program's by a relative error of at most 0.0095.
Values may be sent and summed in bfloat16 or wider, within the bound.
A program may use at most 64 MiB of HBM per device.

v0:
```python
import jax
import jax.numpy as jnp
from jax import lax
from jax.sharding import PartitionSpec as P

step_user = 0.05
step_item = 0.004
shrinkage = 0.05


def shifted(x, axis, by):
    peers = lax.axis_size(axis)
    return lax.ppermute(x, axis, [(i, (i + by) % peers) for i in range(peers)])


def unpack_mask(words):
    shifts = jnp.arange(8, dtype=jnp.int32)
    bits = jnp.bitwise_and(jnp.right_shift(words[:, :, None, :], shifts[None, None, :, None]), 1)
    return bits.reshape(words.shape[0], words.shape[1] * 8, words.shape[2]).astype(jnp.float32)


def device_terms(users, panel_low, blocks, count, rates, words):
    tile_side = rates.shape[-1]
    width = users.shape[1]
    user_count = users.shape[0] // tile_side
    item_count = panel_low.shape[0] // tile_side
    live = (jnp.arange(blocks.shape[0], dtype=jnp.int32) < count).astype(jnp.float32)
    weights = unpack_mask(words) * live[:, None, None]
    user_rows = jnp.take(users.reshape(user_count, tile_side, width), blocks[:, 0], axis=0)
    item_rows = jnp.take(panel_low.reshape(item_count, tile_side, width), blocks[:, 1], axis=0)
    predicted = jnp.einsum("kur,kir->kui", user_rows, item_rows, preferred_element_type=jnp.float32)
    error_tile = (weights * (rates.astype(jnp.float32) - predicted)).astype(jnp.bfloat16)
    user_terms = jnp.einsum(
        "kui,kir->kur", error_tile, item_rows, preferred_element_type=jnp.float32
    )
    item_terms = jnp.einsum(
        "kui,kur->kir", error_tile, user_rows, preferred_element_type=jnp.float32
    )
    user_hot = (blocks[:, 0][:, None] == jnp.arange(user_count, dtype=jnp.int32)[None, :]).astype(
        jnp.float32
    )
    item_hot = (blocks[:, 1][:, None] == jnp.arange(item_count, dtype=jnp.int32)[None, :]).astype(
        jnp.float32
    )
    grad_user = jnp.einsum(
        "kb,kur->bur", user_hot, user_terms, precision=lax.Precision.HIGHEST
    ).reshape(-1, width)
    grad_item = jnp.einsum(
        "kb,kir->bir", item_hot, item_terms, precision=lax.Precision.HIGHEST
    ).reshape(-1, width)
    return (grad_user, grad_item)


def shards(user_factors, item_factors, tile_blocks, tile_counts, ratings, mask_words):
    blocks_all = tile_blocks[0, 0]
    counts_all = tile_counts[0, 0]
    rates_all = ratings[0, 0]
    words_all = mask_words[0, 0]
    visits = counts_all.shape[0]
    users = user_factors
    panel = item_factors
    for visit in range(visits):
        panel_low = lax.all_gather(panel.astype(jnp.bfloat16), "shard", axis=0, tiled=True)
        grad_user, grad_item = device_terms(
            users,
            panel_low,
            blocks_all[visit],
            counts_all[visit],
            rates_all[visit],
            words_all[visit],
        )
        summed = lax.psum_scatter(
            grad_item.astype(jnp.bfloat16), "shard", scatter_dimension=0, tiled=True
        ).astype(jnp.float32)
        factor = users.astype(jnp.float32)
        users = (factor + step_user * (grad_user - shrinkage * factor)).astype(jnp.bfloat16)
        panel = panel + step_item * (summed - shrinkage * panel)
        if visit + 1 < visits:
            panel = shifted(panel.astype(jnp.bfloat16), "strata", 1).astype(panel.dtype)
    return (users, panel)


def solution(mesh):
    placed = (
        P(("strata", "shard"), None),
        P(("strata", "shard"), None),
        P("strata", "shard", None, None, None),
        P("strata", "shard", None),
        P("strata", "shard", None, None, None, None),
        P("strata", "shard", None, None, None, None),
    )
    return jax.shard_map(
        shards,
        mesh=mesh,
        in_specs=placed,
        out_specs=(P(("strata", "shard"), None), P(("strata", "shard"), None)),
        check_vma=False,
    )
```

profile of v0, /device:TPU:32, one launch (start us, length us, event | category | flops | bytes accessed | tf_op | source)
XLA Modules:
  0.0 393.6 jit_solution(7805216325913225970)
XLA Ops:
  9.1 1.4 fusion.83
  10.6 1.2 compare_convert_fusion.2
  13.2 1.5 slice_bitcast_fusion
  14.7 26.6 %all_gather.9 = bf16[512,512]{1,0:T(8,128)(2,1)S(1)} all-gather(bf16[32,512]{1,0:T(8,128)(2,1)S(1)} %convert_element_type.130), channel_id=1, replica_groups=mesh['strata'=32,'shard'=16] {'shard'}, dimensions={0}, use_global_device_ids=true | all-gather | bytes 557056 | tf_op jit(solution)/shard_map/all_gather | solution.py:63
  42.7 1.5 fusion.35
  44.8 2.2 fusion.21
  47.0 0.9 copy.9
  48.5 2.2 fusion.19
  50.8 1.2 copy.8
  52.5 83.5 %reduce-scatter.4.cloned.1.call-done = bf16[32,512]{1,0:T(8,128)(2,1)} async-done(((bf16[512,512]{1,0:T(8,128)(2,1)}), bf16[32,512]{1,0:T(8,128)(2,1)}) %reduce-scatter.4.cloned.1.call-update) | async-done | bytes 32784 | tf_op jit(solution)/shard_map/reduce_scatter | solution.py:72
  136.8 2.8 collective-permute-start
  140.2 1.6 gather_fusion.2
  141.8 1.7 collective-permute-done
  143.5 24.0 %all_gather.10 = bf16[512,512]{1,0:T(8,128)(2,1)S(1)} all-gather(bf16[32,512]{1,0:T(8,128)(2,1)S(1)} %collective-permute-done), channel_id=1, replica_groups=mesh['strata'=32,'shard'=16] {'shard'}, dimensions={0}, use_global_device_ids=true | all-gather | bytes 557056 | tf_op jit(solution)/shard_map/all_gather | solution.py:63
  168.1 1.9 fusion.34
  170.5 2.2 fusion.24
  172.8 0.9 copy.11
  174.9 2.2 fusion.15
  177.1 2.5 copy.10
  179.7 81.1 %reduce-scatter.6.cloned.1.call-done = bf16[32,512]{1,0:T(8,128)(2,1)} async-done(((bf16[512,512]{1,0:T(8,128)(2,1)}), bf16[32,512]{1,0:T(8,128)(2,1)}) %reduce-scatter.6.cloned.1.call-update) | async-done | bytes 32784 | tf_op jit(solution)/shard_map/reduce_scatter | solution.py:72
  261.5 2.8 collective-permute-start.1
  264.4 2.0 fusion.5
  266.4 1.6 gather_fusion.4
  268.3 24.7 %all_gather.11 = bf16[512,512]{1,0:T(8,128)(2,1)S(1)} all-gather(bf16[32,512]{1,0:T(8,128)(2,1)S(1)} %collective-permute-done.1), channel_id=1, replica_groups=mesh['strata'=32,'shard'=16] {'shard'}, dimensions={0}, use_global_device_ids=true | all-gather | bytes 557056 | tf_op jit(solution)/shard_map/all_gather | solution.py:63
  293.6 1.9 fusion.33
  296.0 2.2 fusion.27
  298.2 0.9 copy.13
  299.7 2.2 fusion.11
  301.9 1.2 copy.12
  303.1 1.4 fusion.8
  304.6 81.1 %reduce-scatter.8.cloned.1.call-done = bf16[32,512]{1,0:T(8,128)(2,1)} async-done(((bf16[512,512]{1,0:T(8,128)(2,1)}), bf16[32,512]{1,0:T(8,128)(2,1)}) %reduce-scatter.8.cloned.1.call-update) | async-done | bytes 32784 | tf_op jit(solution)/shard_map/reduce_scatter | solution.py:72
  385.7 1.4 convert_add_fusion.3
  (50 shorter events, 12.7 us)
Async XLA Ops:
  7.2 34.9 %copy-start.2 = (bf16[1024,512]{1,0:T(8,128)(2,1)S(1)}, bf16[1024,512]{1,0:T(8,128)(2,1)}, u32[]{:S(2)}) copy-start(bf16[1024,512]{1,0:T(8,128)(2,1)} %param.10) | copy-start | bytes 3145732
  7.2 128.8 %reduce-scatter.4.cloned.1.call-start = ((), (), s32[]{:S(2)}) async-start(), calls=%async_computation.3 | async-start | bytes 557056 | tf_op jit(solution)/shard_map/reduce_scatter | solution.py:72
  42.7 1.5 copy-start.5
  44.2 0.6 copy-start.6
  44.8 3.2 copy-start.4
  48.0 212.8 %reduce-scatter.6.cloned.1.call-start = ((), (), s32[]{:S(2)}) async-start(), calls=%async_computation.4 | async-start | bytes 557056 | tf_op jit(solution)/shard_map/reduce_scatter | solution.py:72
  52.0 84.0 %copy-start.3 = (f32[32,512]{1,0:T(8,128)S(1)}, f32[32,512]{1,0:T(8,128)}, u32[]{:S(2)}) copy-start(f32[32,512]{1,0:T(8,128)} %param.11) | copy-start | bytes 196612
  136.8 6.7 %collective-permute-start = (bf16[32,512]{1,0:T(8,128)(2,1)S(1)}, bf16[32,512]{1,0:T(8,128)(2,1)S(1)}, u32[]{:S(2)}, u32[]{:S(2)}) collective-permute-start(bf16[32,512]{1,0:T(8,128)(2,1)S(1)} %add_convert_fusion), channel_id=1, source_target_pairs={{0,16},{16,32},{32,48},{48,64},{64,80},{80,96},{96,112},{112,128},... | collective-permute-start | bytes 98312 | tf_op jit(solution)/shard_map/ppermute | solution.py:13
  140.2 27.9 %copy-start.7 = (s32[128]{0:T(128)S(1)}, s32[128]{0:T(128)}, u32[]{:S(2)}) copy-start(s32[128]{0:T(128)} %shift_right_arithmetic.70) | copy-start | bytes 1540
  168.1 1.9 copy-start.1
  173.7 212.0 %reduce-scatter.8.cloned.1.call-start = ((), (), s32[]{:S(2)}) async-start(), calls=%async_computation.5 | async-start | bytes 557056 | tf_op jit(solution)/shard_map/reduce_scatter | solution.py:72
  261.5 6.7 %collective-permute-start.1 = (bf16[32,512]{1,0:T(8,128)(2,1)S(1)}, bf16[32,512]{1,0:T(8,128)(2,1)S(1)}, u32[]{:S(2)}, u32[]{:S(2)}) collective-permute-start(bf16[32,512]{1,0:T(8,128)(2,1)S(1)} %fusion.53), channel_id=1, source_target_pairs={{0,16},{16,32},{32,48},{48,64},{64,80},{80,96},{96,112},{112,128},... | collective-permute-start | bytes 98312 | tf_op jit(solution)/shard_map/ppermute | solution.py:13
  293.6 1.9 copy-start
Sparse Core Ops, SparseCore 0:
  48.1 87.8 reduce-scatter.3
  173.8 86.9 reduce-scatter.5
  299.3 86.3 reduce-scatter.7
where the time goes:
time: 394 us
  waiting for transfers between devices  248 us (63%)
  blocking collectives  75.3 us (19%)
  matrix products  21.6 us (5%)
  local copies, waits for them, and re-layouts  18.3 us (5%)
  between operations  14.1 us (4%)
  other arithmetic  10.7 us (3%)
  starting transfers between devices  5.75 us (1%)
    reduce_scatter x3, waiting for transfers between devices, shards(): lax.psum_scatter(grad_item.astype(jnp.bfloat16), 'shard', scatter_dimensi...  246 us
    all_gather x3, blocking collectives, shards(): lax.all_gather(panel.astype(jnp.bfloat16), 'shard', axis=0, tiled=True)  75.3 us
  transfers between devices with their start and end apart: 5, of which 5 were waited for; matrix products, arithmetic and copies ran while one was open for 5% of the time, Pallas kernels for 0%

commit v1 on v0

--- a/solution.py
+++ b/solution.py
@@ -60,7 +60,12 @@
     users = user_factors
     panel = item_factors
     for visit in range(visits):
-        panel_low = lax.all_gather(panel.astype(jnp.bfloat16), "shard", axis=0, tiled=True)
+        panel_low = jnp.concatenate(
+            lax.all_to_all(
+                jnp.stack([panel.astype(jnp.bfloat16)] * lax.axis_size("shard")), "shard", 0, 0
+            ),
+            axis=0,
+        )
         grad_user, grad_item = device_terms(
             users,
             panel_low,

time: 394 us -> 370 us (0.939)
  blocking collectives: 75.3 us -> 0 us
  waiting for transfers between devices: 248 us -> 283 us
  starting transfers between devices: 5.75 us -> 22.7 us
    all_gather x3 -> x0, blocking collectives: 75.3 us -> none  [shards(): lax.all_gather(panel.astype(jnp.bfloat16), 'shard', axis=0, tiled=True)]
    all_to_all x0 -> x3, waiting for transfers between devices: none -> 22.2 us  [shards(): lax.all_to_all(jnp.stack([panel.astype(jnp.bfloat16)] * lax.axis_size('sh...]
    all_to_all x0 -> x3, starting transfers between devices: none -> 16.5 us  [shards(): lax.all_to_all(jnp.stack([panel.astype(jnp.bfloat16)] * lax.axis_size('sh...]
    reduce_scatter x3, waiting for transfers between devices: 246 us -> 255 us  [shards(): lax.psum_scatter(grad_item.astype(jnp.bfloat16), 'shard', scatter_dimensi...]
  transfers between devices with their start and end apart: 5 -> 8, of which waited for: 5 -> 8; matrix products, arithmetic and copies ran while one was open for 5% -> 6% of each run, Pallas kernels for 0% -> 0%
where the time goes in v1:
time: 370 us; the launch traced here: 369 us
  waiting for transfers between devices  283 us (76%)
  starting transfers between devices  22.7 us (6%)
  matrix products  22.7 us (6%)
  local copies, waits for them, and re-layouts  17.5 us (5%)
  between operations  14.2 us (4%)
  other arithmetic  8.72 us (2%)
    reduce_scatter x3, waiting for transfers between devices, shards(): lax.psum_scatter(grad_item.astype(jnp.bfloat16), 'shard', scatter_dimensi...  255 us
    all_to_all x3, waiting for transfers between devices, shards(): lax.all_to_all(jnp.stack([panel.astype(jnp.bfloat16)] * lax.axis_size('sh...  22.2 us
    all_to_all x3, starting transfers between devices, shards(): lax.all_to_all(jnp.stack([panel.astype(jnp.bfloat16)] * lax.axis_size('sh...  16.5 us
  transfers between devices with their start and end apart: 8, of which 8 were waited for; matrix products, arithmetic and copies ran while one was open for 6% of the time, Pallas kernels for 0%

profile of v1, /device:TPU:32, one launch (start us, length us, event | category | flops | bytes accessed | tf_op | source)
XLA Modules:
  0.0 368.7 jit_solution(12400106865358108150)
XLA Ops:
  9.0 7.0 %all-to-all-start = ((bf16[16,32,512]{2,1,0:T(8,128)(2,1)}), bf16[16,32,512]{2,1,0:T(8,128)(2,1)S(1)}, u32[]{:S(2)}, u32[]{:S(2)}) async-start(bf16[16,32,512]{2,1,0:T(8,128)(2,1)} %stack.6), calls=%async_computation | async-start | bytes 1048576 | tf_op jit(solution)/shard_map/all_to_all | solution.py:64
  16.1 1.4 fusion.83
  20.2 8.1 %all-to-all-done = bf16[16,32,512]{2,1,0:T(8,128)(2,1)S(1)} async-done(((bf16[16,32,512]{2,1,0:T(8,128)(2,1)}), bf16[16,32,512]{2,1,0:T(8,128)(2,1)S(1)}, u32[]{:S(2)}, u32[]{:S(2)}) %all-to-all-start) | async-done | bytes 524320 | tf_op jit(solution)/shard_map/all_to_all | solution.py:64
  29.0 1.5 fusion.35
  31.0 2.2 fusion.21
  34.1 1.2 compare_convert_fusion.1
  35.4 87.1 %reduce-scatter.4.cloned.1.call-done = bf16[32,512]{1,0:T(8,128)(2,1)} async-done(((bf16[512,512]{1,0:T(8,128)(2,1)}), bf16[32,512]{1,0:T(8,128)(2,1)}) %reduce-scatter.4.cloned.1.call-update) | async-done | bytes 32784 | tf_op jit(solution)/shard_map/reduce_scatter | solution.py:77
  123.3 2.8 collective-permute-start
  126.6 3.4 collective-permute-done
  130.8 4.7 %all-to-all-start.1 = ((bf16[16,32,512]{2,1,0:T(8,128)(2,1)}), bf16[16,32,512]{2,1,0:T(8,128)(2,1)S(1)}, u32[]{:S(2)}, u32[]{:S(2)}) async-start(bf16[16,32,512]{2,1,0:T(8,128)(2,1)} %stack.7), calls=%async_computation.2 | async-start | bytes 1048576 | tf_op jit(solution)/shard_map/all_to_all | solution.py:64
  135.8 2.2 fusion.19
  138.0 1.2 copy.8
  139.8 1.6 gather_fusion.2
  141.3 6.5 %all-to-all-done.1 = bf16[16,32,512]{2,1,0:T(8,128)(2,1)S(1)} async-done(((bf16[16,32,512]{2,1,0:T(8,128)(2,1)}), bf16[16,32,512]{2,1,0:T(8,128)(2,1)S(1)}, u32[]{:S(2)}, u32[]{:S(2)}) %all-to-all-start.1) | async-done | bytes 524320 | tf_op jit(solution)/shard_map/all_to_all | solution.py:64
  148.6 2.2 fusion.34
  151.3 2.2 fusion.24
  155.0 86.4 %reduce-scatter.6.cloned.1.call-done = bf16[32,512]{1,0:T(8,128)(2,1)} async-done(((bf16[512,512]{1,0:T(8,128)(2,1)}), bf16[32,512]{1,0:T(8,128)(2,1)}) %reduce-scatter.6.cloned.1.call-update) | async-done | bytes 32784 | tf_op jit(solution)/shard_map/reduce_scatter | solution.py:77
  242.2 2.8 collective-permute-start.1
  245.0 1.7 fusion.48
  246.7 2.2 collective-permute-done.1
  249.7 4.8 %all-to-all-start.2 = ((bf16[16,32,512]{2,1,0:T(8,128)(2,1)}), bf16[16,32,512]{2,1,0:T(8,128)(2,1)}, u32[]{:S(2)}, u32[]{:S(2)}) async-start(bf16[16,32,512]{2,1,0:T(8,128)(2,1)} %stack.8), calls=%async_computation.4 | async-start | bytes 1048576 | tf_op jit(solution)/shard_map/all_to_all | solution.py:64
  254.8 2.2 fusion.15
  257.0 1.2 copy.10
  259.3 7.6 %all-to-all-done.2 = bf16[16,32,512]{2,1,0:T(8,128)(2,1)} async-done(((bf16[16,32,512]{2,1,0:T(8,128)(2,1)}), bf16[16,32,512]{2,1,0:T(8,128)(2,1)}, u32[]{:S(2)}, u32[]{:S(2)}) %all-to-all-start.2) | async-done | bytes 524320 | tf_op jit(solution)/shard_map/all_to_all | solution.py:64
  266.9 1.7 gather_fusion.5
  268.6 1.5 fusion.33
  270.6 2.2 fusion.27
  274.2 2.2 fusion.11
  276.5 1.2 copy.12
  277.7 1.4 fusion.8
  279.1 81.7 %reduce-scatter.8.cloned.1.call-done = bf16[32,512]{1,0:T(8,128)(2,1)} async-done(((bf16[512,512]{1,0:T(8,128)(2,1)}), bf16[32,512]{1,0:T(8,128)(2,1)}) %reduce-scatter.8.cloned.1.call-update) | async-done | bytes 32784 | tf_op jit(solution)/shard_map/reduce_scatter | solution.py:77
  360.8 1.4 convert_add_fusion.3
  (56 shorter events, 16.9 us)
Async XLA Ops:
  7.2 11.8 %copy-start.2 = (bf16[1024,512]{1,0:T(8,128)(2,1)S(1)}, bf16[1024,512]{1,0:T(8,128)(2,1)}, u32[]{:S(2)}) copy-start(bf16[1024,512]{1,0:T(8,128)(2,1)} %param.10) | copy-start | bytes 3145732
  7.2 12.4 %copy-start.5 = (s32[1,1,3,8,16,128]{5,4,3,2,1,0:T(8,128)S(1)}, s32[1,1,3,8,16,128]{5,4,3,2,1,0:T(8,128)}, u32[]{:S(2)}) copy-start(s32[1,1,3,8,16,128]{5,4,3,2,1,0:T(8,128)} %param.15) | copy-start | bytes 589828
  9.0 19.4 %all-to-all-start = ((bf16[16,32,512]{2,1,0:T(8,128)(2,1)}), bf16[16,32,512]{2,1,0:T(8,128)(2,1)S(1)}, u32[]{:S(2)}, u32[]{:S(2)}) async-start(bf16[16,32,512]{2,1,0:T(8,128)(2,1)} %stack.6), calls=%async_computation | async-start | bytes 1048576 | tf_op jit(solution)/shard_map/all_to_all | solution.py:64
  16.0 106.5 %reduce-scatter.4.cloned.1.call-start = ((), (), s32[]{:S(2)}) async-start(), calls=%async_computation.6 | async-start | bytes 557056 | tf_op jit(solution)/shard_map/reduce_scatter | solution.py:77
  31.0 91.5 %copy-start.4 = (f32[32,512]{1,0:T(8,128)S(1)}, f32[32,512]{1,0:T(8,128)}, u32[]{:S(2)}) copy-start(f32[32,512]{1,0:T(8,128)} %param.11) | copy-start | bytes 196612
  123.3 6.7 %collective-permute-start = (bf16[32,512]{1,0:T(8,128)(2,1)S(1)}, bf16[32,512]{1,0:T(8,128)(2,1)S(1)}, u32[]{:S(2)}, u32[]{:S(2)}) collective-permute-start(bf16[32,512]{1,0:T(8,128)(2,1)S(1)} %add_convert_fusion), channel_id=1, source_target_pairs={{0,16},{16,32},{32,48},{48,64},{64,80},{80,96},{96,112},{112,128},... | collective-permute-start | bytes 98312 | tf_op jit(solution)/shard_map/ppermute | solution.py:13
  130.8 17.0 %all-to-all-start.1 = ((bf16[16,32,512]{2,1,0:T(8,128)(2,1)}), bf16[16,32,512]{2,1,0:T(8,128)(2,1)S(1)}, u32[]{:S(2)}, u32[]{:S(2)}) async-start(bf16[16,32,512]{2,1,0:T(8,128)(2,1)} %stack.7), calls=%async_computation.2 | async-start | bytes 1048576 | tf_op jit(solution)/shard_map/all_to_all | solution.py:64
  135.6 105.9 %reduce-scatter.6.cloned.1.call-start = ((), (), s32[]{:S(2)}) async-start(), calls=%async_computation.7 | async-start | bytes 557056 | tf_op jit(solution)/shard_map/reduce_scatter | solution.py:77
  138.0 1.2 copy-start.3
  139.7 8.8 %copy-start.6 = (s32[8,16,128]{2,1,0:T(8,128)S(1)}, s32[8,16,128]{2,1,0:T(8,128)}, u32[]{:S(2)}) copy-start(s32[8,16,128]{2,1,0:T(8,128)} %get-tuple-element.18) | copy-start | bytes 196612
  139.7 8.8 %copy-start.7 = (f32[8]{0:T(128)S(1)}, f32[8]{0:T(128)}, u32[]{:S(2)}) copy-start(f32[8]{0:T(128)} %compare_convert_fusion.1) | copy-start | bytes 100
  148.5 5.9 %copy-start = (bf16[8,128,512]{2,1,0:T(8,128)(2,1)}, bf16[8,128,512]{2,1,0:T(8,128)(2,1)S(1)}, u32[]{:S(2)}) copy-start(bf16[8,128,512]{2,1,0:T(8,128)(2,1)S(1)} %gather_fusion.3) | copy-start | bytes 3145732
  148.5 2.2 copy-start.1
  242.2 6.7 %collective-permute-start.1 = (bf16[32,512]{1,0:T(8,128)(2,1)S(1)}, bf16[32,512]{1,0:T(8,128)(2,1)S(1)}, u32[]{:S(2)}, u32[]{:S(2)}) collective-permute-start(bf16[32,512]{1,0:T(8,128)(2,1)S(1)} %fusion.53), channel_id=1, source_target_pairs={{0,16},{16,32},{32,48},{48,64},{64,80},{80,96},{96,112},{112,128},... | collective-permute-start | bytes 98312 | tf_op jit(solution)/shard_map/ppermute | solution.py:13
  249.7 17.2 %all-to-all-start.2 = ((bf16[16,32,512]{2,1,0:T(8,128)(2,1)}), bf16[16,32,512]{2,1,0:T(8,128)(2,1)}, u32[]{:S(2)}, u32[]{:S(2)}) async-start(bf16[16,32,512]{2,1,0:T(8,128)(2,1)} %stack.8), calls=%async_computation.4 | async-start | bytes 1048576 | tf_op jit(solution)/shard_map/all_to_all | solution.py:64
  254.5 106.3 %reduce-scatter.8.cloned.1.call-start = ((), (), s32[]{:S(2)}) async-start(), calls=%async_computation.8 | async-start | bytes 557056 | tf_op jit(solution)/shard_map/reduce_scatter | solution.py:77
Sparse Core Ops, SparseCore 0:
  34.3 88.1 reduce-scatter.3
  154.5 86.8 reduce-scatter.5
  273.9 86.9 reduce-scatter.7
